TPU v7x, 32 devices: a whole 2x2x4 slice. The times are simulated.
32 devices in a mesh: depth: 8 (over z, x), tile: 4 (over y, core).
Axes of the slice: x: 2, y: 2, z: 4, core: 2. Of those that a mesh axis runs over, the one named last changes fastest.
Arguments:
- vorticity: bfloat16 [32, 256, 1024], P('depth', None, 'tile'), may hold values from -6 to 6
- tf_color: float32 [3, 16], replicated, may hold values from 0.05 to 1
- tf_extinction: float32 [16], replicated, may hold values from 0.001 to 10
Outputs:
- final_image: float32 [4, 256, 1024], P(None, 'depth', 'tile')
All inputs are finite; a program needn't handle non-finite values.
Results may differ from a plain program's by a relative error of at most 0.002.
Values may be sent and summed in bfloat16 or wider, within the bound.
A program may use at most 64 MiB of HBM per device.

v0:
```python
import jax
import jax.numpy as jnp
from jax import lax
from jax.sharding import PartitionSpec as P


def extended(cells, sides, width):
    for axis, dim in sides:
        count = lax.axis_size(axis)
        ends = count - 1
        head = lax.slice_in_dim(cells, 0, width, axis=dim)
        tail = lax.slice_in_dim(cells, cells.shape[dim] - width, cells.shape[dim], axis=dim)
        cells = jnp.concatenate(
            [
                lax.ppermute(tail, axis, [(i, (i + 1) % count) for i in range(ends)]),
                cells,
                lax.ppermute(head, axis, [((i + 1) % count, i) for i in range(ends)]),
            ],
            axis=dim,
        )
    return cells


def shade_sample(slab_below, slab_here, slab_above, tf_color, tf_extinction, thickness):
    middle = slab_here.astype(jnp.float32)
    grad_z = 0.5 * (
        slab_above[1:-1, 1:-1].astype(jnp.float32) - slab_below[1:-1, 1:-1].astype(jnp.float32)
    )
    grad_x = 0.5 * (middle[2:, 1:-1] - middle[:-2, 1:-1])
    grad_y = 0.5 * (middle[1:-1, 2:] - middle[1:-1, :-2])
    scalar = middle[1:-1, 1:-1]
    facing = 0.48 * grad_x + 0.6 * grad_y + 0.64 * grad_z
    lighting = 0.55 + 0.45 * facing / jnp.sqrt(
        grad_x * grad_x + grad_y * grad_y + grad_z * grad_z + 0.25
    )
    count_knots = tf_extinction.shape[0]
    position = jnp.clip((scalar + 4.0) * ((count_knots - 1) / 8.0), 0.0, count_knots - 1.0)
    knot_points = jnp.arange(count_knots, dtype=jnp.float32)
    weights = jnp.maximum(0.0, 1.0 - jnp.abs(position[None] - knot_points[:, None, None]))
    colour_mix = jnp.einsum("ck,kxy->cxy", tf_color, weights, precision=lax.Precision.HIGHEST)
    extinction = jnp.einsum("k,kxy->xy", tf_extinction, weights, precision=lax.Precision.HIGHEST)
    opacity = 1.0 - jnp.exp(-extinction * thickness)
    return jnp.concatenate([opacity[None] * lighting[None] * colour_mix, opacity[None]], axis=0)


def composite(nearer, farther):
    return nearer + (1.0 - nearer[3:4]) * farther


def local(vorticity, tf_color, tf_extinction):
    depth_count = lax.axis_size("depth")
    local_slices = vorticity.shape[0]
    tile_rows = vorticity.shape[1]
    tile_cols = vorticity.shape[2]
    thickness = 1.0 / (local_slices * depth_count)
    padded = extended(vorticity, (("depth", 0), ("tile", 2)), 1)
    widened = jnp.pad(padded, ((0, 0), (1, 1), (0, 0)))

    def march(slice_index, accumulated):
        slab_below = lax.dynamic_index_in_dim(widened, slice_index, 0, keepdims=False)
        slab_here = lax.dynamic_index_in_dim(widened, slice_index + 1, 0, keepdims=False)
        slab_above = lax.dynamic_index_in_dim(widened, slice_index + 2, 0, keepdims=False)
        sample = shade_sample(slab_below, slab_here, slab_above, tf_color, tf_extinction, thickness)
        return composite(accumulated, sample)

    blank_image = jnp.zeros((4, tile_rows, tile_cols), jnp.float32)
    partial_value = lax.fori_loop(0, local_slices, march, blank_image)
    block_rows = tile_rows // depth_count
    rounds = depth_count.bit_length() - 1
    stacked = partial_value.reshape(4, 1, tile_rows, tile_cols)
    pieces = lax.all_to_all(
        stacked.astype(jnp.bfloat16), "depth", split_axis=2, concat_axis=1, tiled=True
    ).astype(stacked.dtype)
    for halving in range(rounds):
        paired = pieces.reshape(4, pieces.shape[1] // 2, 2, block_rows, tile_cols)
        pieces = composite(paired[:, :, 0], paired[:, :, 1])
    final_image = pieces[:, 0]
    return final_image


def solution(mesh):
    placed = (P("depth", None, "tile"), P(), P())
    return jax.shard_map(
        local, mesh=mesh, in_specs=placed, out_specs=P(None, "depth", "tile"), check_vma=False
    )
```

profile of v0, /device:TPU:1, one launch (start us, length us, event | category | flops | bytes accessed | tf_op | source)
XLA Modules:
  0.0 76.3 jit_solution(14886004903567915635)
XLA Ops:
  0.0 1.0 %fusion.37 = (bf16[1,256,256]{2,1,0:T(8,128)(2,1)S(1)}, bf16[1,256,256]{2,1,0:T(8,128)(2,1)S(1)}) fusion(bf16[4,256,256]{2,1,0:T(8,128)(2,1)} %param.5), kind=kLoop, calls=%fused_computation.64 | loop fusion | bytes 524288 | tf_op jit(solution)/shard_map/slice | solution.py:11
  1.0 3.9 %collective-permute-start = (bf16[1,256,256]{2,1,0:T(8,128)(2,1)S(1)}, bf16[1,256,256]{2,1,0:T(8,128)(2,1)S(1)}, u32[]{:S(2)}, u32[]{:S(2)}) collective-permute-start(bf16[1,256,256]{2,1,0:T(8,128)(2,1)S(1)} %get-tuple-element.180), channel_id=1, source_target_pairs={{0,4},{4,8},{8,12},{12,16},{16,20},{20,24},{24,28},{1,5},{5,9},{9,... | collective-permute-start | bytes 393224 | tf_op jit(solution)/shard_map/ppermute | solution.py:15
  4.9 1.3 %collective-permute-start.1 = (bf16[1,256,256]{2,1,0:T(8,128)(2,1)S(1)}, bf16[1,256,256]{2,1,0:T(8,128)(2,1)S(1)}, u32[]{:S(2)}, u32[]{:S(2)}) collective-permute-start(bf16[1,256,256]{2,1,0:T(8,128)(2,1)S(1)} %get-tuple-element.179), channel_id=1, source_target_pairs={{4,0},{8,4},{12,8},{16,12},{20,16},{24,20},{28,24},{5,1},{9,5},{13... | collective-permute-start | bytes 393224 | tf_op jit(solution)/shard_map/ppermute | solution.py:17
  6.2 0.9 %collective-permute-done = bf16[1,256,256]{2,1,0:T(8,128)(2,1)S(1)} collective-permute-done((bf16[1,256,256]{2,1,0:T(8,128)(2,1)S(1)}, bf16[1,256,256]{2,1,0:T(8,128)(2,1)S(1)}, u32[]{:S(2)}, u32[]{:S(2)}) %collective-permute-start) | collective-permute-done | bytes 131104 | tf_op jit(solution)/shard_map/ppermute | solution.py:15
  7.1 1.1 %constant_dynamic-update-slice_fusion.1 = bf16[6,256,256]{2,1,0:T(8,128)(2,1)S(1)} fusion(bf16[6,256,256]{2,1,0:T(8,128)(2,1)S(1)} %constant_dynamic-update-slice_fusion.2, bf16[4,256,256]{2,1,0:T(8,128)(2,1)} %param.5), kind=kLoop, calls=%fused_computation.60 | loop fusion | bytes 1048576
  8.2 2.5 %collective-permute-done.1 = bf16[1,256,256]{2,1,0:T(8,128)(2,1)S(1)} collective-permute-done((bf16[1,256,256]{2,1,0:T(8,128)(2,1)S(1)}, bf16[1,256,256]{2,1,0:T(8,128)(2,1)S(1)}, u32[]{:S(2)}, u32[]{:S(2)}) %collective-permute-start.1) | collective-permute-done | bytes 131104 | tf_op jit(solution)/shard_map/ppermute | solution.py:17
  10.7 0.2 fusion.35
  10.9 5.1 %collective-permute-start.2 = (bf16[6,256,1]{2,1,0:T(8,128)(2,1)S(1)}, bf16[6,256,1]{2,1,0:T(8,128)(2,1)S(1)}, u32[]{:S(2)}, u32[]{:S(2)}) collective-permute-start(bf16[6,256,1]{2,1,0:T(8,128)(2,1)S(1)} %get-tuple-element.175), channel_id=1, source_target_pairs={{0,1},{1,2},{2,3},{4,5},{5,6},{6,7},{8,9},{9,10},{10,11},{12,13},{... | collective-permute-start | bytes 9224 | tf_op jit(solution)/shard_map/ppermute | solution.py:15
  16.0 1.9 %collective-permute-start.3 = (bf16[6,256,1]{2,1,0:T(8,128)(2,1)S(1)}, bf16[6,256,1]{2,1,0:T(8,128)(2,1)}, u32[]{:S(2)}, u32[]{:S(2)}) collective-permute-start(bf16[6,256,1]{2,1,0:T(8,128)(2,1)S(1)} %get-tuple-element.176), channel_id=1, source_target_pairs={{1,0},{2,1},{3,2},{5,4},{6,5},{7,6},{9,8},{10,9},{11,10},{13,12},{... | collective-permute-start | bytes 9224 | tf_op jit(solution)/shard_map/ppermute | solution.py:17
  18.0 0.0 copy-start
  18.0 0.0 copy-start.1
  18.0 2.7 %collective-permute-done.2 = bf16[6,256,1]{2,1,0:T(8,128)(2,1)S(1)} collective-permute-done((bf16[6,256,1]{2,1,0:T(8,128)(2,1)S(1)}, bf16[6,256,1]{2,1,0:T(8,128)(2,1)S(1)}, u32[]{:S(2)}, u32[]{:S(2)}) %collective-permute-start.2) | collective-permute-done | bytes 3104 | tf_op jit(solution)/shard_map/ppermute | solution.py:15
  20.7 4.5 %collective-permute-done.3 = bf16[6,256,1]{2,1,0:T(8,128)(2,1)} collective-permute-done((bf16[6,256,1]{2,1,0:T(8,128)(2,1)S(1)}, bf16[6,256,1]{2,1,0:T(8,128)(2,1)}, u32[]{:S(2)}, u32[]{:S(2)}) %collective-permute-start.3) | collective-permute-done | bytes 3104 | tf_op jit(solution)/shard_map/ppermute | solution.py:17
  25.2 2.0 %fusion.27 = bf16[6,258,258]{2,1,0:T(8,128)(2,1)S(1)} fusion(bf16[6,256,1]{2,1,0:T(8,128)(2,1)} %collective-permute-done.3, bf16[6,256,256]{2,1,0:T(8,128)(2,1)S(1)} %constant_dynamic-update-slice_fusion, bf16[6,256,1]{2,1,0:T(8,128)(2,1)S(1)} %collective-permute-done.2), kind=kLoop, calls=%fused_computation.42 | loop fusion | flops 4792608 | bytes 1591344 | tf_op jit(solution)/shard_map/concatenate | solution.py:13
  27.3 0.0 copy-done
  27.3 0.0 copy-done.1
  27.3 32.3 %while.16 = (s32[]{:T(128)}, f32[4,256,256]{2,0,1:T(4,128)S(1)}, bf16[6,258,258]{2,1,0:T(8,128)(2,1)S(1)}, f32[16]{0:T(128)S(1)}, f32[3,16]{1,0:T(4,128)S(1)}, /...) while((s32[]{:T(128)}, f32[4,256,256]{2,0,1:T(4,128)S(1)}, ...), condition=%wide.region_1.2_spmd.clone, body=%wide.region_0.1_spmd.clone.sunk | while | flops 62260236 | bytes 12466700 | solution.py:67
  27.3 0.1 dynamic-slice_bitcast_fusion.3
  27.4 0.1 fusion.46
  27.5 2.8 %fusion.47 = f32[1,256,256]{2,0,1:T(1,128)S(1)} fusion(f32[256,256]{1,0:T(8,128)S(1)} %fusion.46, f32[16]{0:T(128)S(1)} %get-tuple-element.245), kind=kOutput, calls=%fused_computation.2.clone.1 | convolution fusion | flops 16777216 | bytes 524352 | tf_op jit(solution)/shard_map/while/body/eval_jaxpr/k,kxy->xy/dot_general | solution.py:41
  30.3 0.5 add_multiply_fusion.2
  30.8 0.2 broadcast_in_dim.26
  31.0 2.9 %fusion.48 = f32[3,256,256]{2,0,1:T(4,128)S(1)} fusion(f32[256,256]{1,0:T(8,128)S(1)} %fusion.46, f32[256,256]{1,0:T(8,128)S(1)} %get-tuple-element.221, f32[3,16]{1,0:T(4,128)S(1)} %get-tuple-element.246), kind=kOutput, calls=%fused_computation.10.clone.1 | convolution fusion | flops 42139648 | bytes 1310912 | tf_op jit(solution)/shard_map/while/body/eval_jaxpr/ck,kxy->cxy/dot_general | solution.py:40
  33.9 0.2 broadcast_select_fusion.2
  34.2 0.3 slice_subtract_fusion.7
  34.5 0.8 %fusion.49 = f32[4,256,256]{2,0,1:T(4,128)S(1)} fusion(f32[1,256,256]{2,0,1:T(1,128)S(1)} %broadcast_in_dim.26, f32[3,256,256]{2,0,1:T(4,128)S(1)} %fusion.48, f32[256,256]{1,0:T(8,128)S(1)} %bitcast.81, f32[4,256,256]{2,0,1:T(4,128)S(1)} %get-tuple-element.233, pred[]{:T(512)S(6)} %compare.44), kind=kLoop, calls=%fused_computation.12.clone.1 | loop fusion | flops 1048576 | bytes 3407873 | tf_op jit(solution)/shard_map/while/body/eval_jaxpr/add | solution.py:47
  35.4 0.1 dynamic-slice_bitcast_fusion.3
  35.5 0.1 fusion.46
  35.6 2.8 %fusion.47 = f32[1,256,256]{2,0,1:T(1,128)S(1)} fusion(f32[256,256]{1,0:T(8,128)S(1)} %fusion.46, f32[16]{0:T(128)S(1)} %get-tuple-element.245), kind=kOutput, calls=%fused_computation.2.clone.1 | convolution fusion | flops 16777216 | bytes 524352 | tf_op jit(solution)/shard_map/while/body/eval_jaxpr/k,kxy->xy/dot_general | solution.py:41
  38.4 0.5 add_multiply_fusion.2
  38.9 0.2 broadcast_in_dim.26
  39.1 2.9 %fusion.48 = f32[3,256,256]{2,0,1:T(4,128)S(1)} fusion(f32[256,256]{1,0:T(8,128)S(1)} %fusion.46, f32[256,256]{1,0:T(8,128)S(1)} %get-tuple-element.221, f32[3,16]{1,0:T(4,128)S(1)} %get-tuple-element.246), kind=kOutput, calls=%fused_computation.10.clone.1 | convolution fusion | flops 42139648 | bytes 1310912 | tf_op jit(solution)/shard_map/while/body/eval_jaxpr/ck,kxy->cxy/dot_general | solution.py:40
  42.0 0.2 broadcast_select_fusion.2
  42.2 0.3 slice_subtract_fusion.7
  42.6 0.8 %fusion.49 = f32[4,256,256]{2,0,1:T(4,128)S(1)} fusion(f32[1,256,256]{2,0,1:T(1,128)S(1)} %broadcast_in_dim.26, f32[3,256,256]{2,0,1:T(4,128)S(1)} %fusion.48, f32[256,256]{1,0:T(8,128)S(1)} %bitcast.81, f32[4,256,256]{2,0,1:T(4,128)S(1)} %get-tuple-element.233, pred[]{:T(512)S(6)} %compare.44), kind=kLoop, calls=%fused_computation.12.clone.1 | loop fusion | flops 1048576 | bytes 3407873 | tf_op jit(solution)/shard_map/while/body/eval_jaxpr/add | solution.py:47
  43.5 0.1 dynamic-slice_bitcast_fusion.3
  43.5 0.1 fusion.46
  43.7 2.8 %fusion.47 = f32[1,256,256]{2,0,1:T(1,128)S(1)} fusion(f32[256,256]{1,0:T(8,128)S(1)} %fusion.46, f32[16]{0:T(128)S(1)} %get-tuple-element.245), kind=kOutput, calls=%fused_computation.2.clone.1 | convolution fusion | flops 16777216 | bytes 524352 | tf_op jit(solution)/shard_map/while/body/eval_jaxpr/k,kxy->xy/dot_general | solution.py:41
  46.5 0.5 add_multiply_fusion.2
  47.0 0.2 broadcast_in_dim.26
  47.1 2.9 %fusion.48 = f32[3,256,256]{2,0,1:T(4,128)S(1)} fusion(f32[256,256]{1,0:T(8,128)S(1)} %fusion.46, f32[256,256]{1,0:T(8,128)S(1)} %get-tuple-element.221, f32[3,16]{1,0:T(4,128)S(1)} %get-tuple-element.246), kind=kOutput, calls=%fused_computation.10.clone.1 | convolution fusion | flops 42139648 | bytes 1310912 | tf_op jit(solution)/shard_map/while/body/eval_jaxpr/ck,kxy->cxy/dot_general | solution.py:40
  50.1 0.2 broadcast_select_fusion.2
  50.3 0.3 slice_subtract_fusion.7
  50.7 0.8 %fusion.49 = f32[4,256,256]{2,0,1:T(4,128)S(1)} fusion(f32[1,256,256]{2,0,1:T(1,128)S(1)} %broadcast_in_dim.26, f32[3,256,256]{2,0,1:T(4,128)S(1)} %fusion.48, f32[256,256]{1,0:T(8,128)S(1)} %bitcast.81, f32[4,256,256]{2,0,1:T(4,128)S(1)} %get-tuple-element.233, pred[]{:T(512)S(6)} %compare.44), kind=kLoop, calls=%fused_computation.12.clone.1 | loop fusion | flops 1048576 | bytes 3407873 | tf_op jit(solution)/shard_map/while/body/eval_jaxpr/add | solution.py:47
  51.5 0.1 dynamic-slice_bitcast_fusion.3
  51.6 0.1 fusion.46
  51.8 2.8 %fusion.47 = f32[1,256,256]{2,0,1:T(1,128)S(1)} fusion(f32[256,256]{1,0:T(8,128)S(1)} %fusion.46, f32[16]{0:T(128)S(1)} %get-tuple-element.245), kind=kOutput, calls=%fused_computation.2.clone.1 | convolution fusion | flops 16777216 | bytes 524352 | tf_op jit(solution)/shard_map/while/body/eval_jaxpr/k,kxy->xy/dot_general | solution.py:41
  54.5 0.5 add_multiply_fusion.2
  55.0 0.2 broadcast_in_dim.26
  55.2 2.9 %fusion.48 = f32[3,256,256]{2,0,1:T(4,128)S(1)} fusion(f32[256,256]{1,0:T(8,128)S(1)} %fusion.46, f32[256,256]{1,0:T(8,128)S(1)} %get-tuple-element.221, f32[3,16]{1,0:T(4,128)S(1)} %get-tuple-element.246), kind=kOutput, calls=%fused_computation.10.clone.1 | convolution fusion | flops 42139648 | bytes 1310912 | tf_op jit(solution)/shard_map/while/body/eval_jaxpr/ck,kxy->cxy/dot_general | solution.py:40
  58.1 0.2 broadcast_select_fusion.2
  58.4 0.3 slice_subtract_fusion.7
  58.8 0.8 %fusion.49 = f32[4,256,256]{2,0,1:T(4,128)S(1)} fusion(f32[1,256,256]{2,0,1:T(1,128)S(1)} %broadcast_in_dim.26, f32[3,256,256]{2,0,1:T(4,128)S(1)} %fusion.48, f32[256,256]{1,0:T(8,128)S(1)} %bitcast.81, f32[4,256,256]{2,0,1:T(4,128)S(1)} %get-tuple-element.233, pred[]{:T(512)S(6)} %compare.44), kind=kLoop, calls=%fused_computation.12.clone.1 | loop fusion | flops 1048576 | bytes 3407873 | tf_op jit(solution)/shard_map/while/body/eval_jaxpr/add | solution.py:47
  59.6 0.2 convert_bitcast_fusion
  59.8 15.3 %all_to_all.4 = bf16[4,1,256,256]{3,0,1,2:T(4,128)(2,1)S(1)} all-to-all(bf16[4,1,256,256]{3,0,1,2:T(4,128)(2,1)S(1)} %convert_bitcast_fusion), channel_id=1, replica_groups=mesh['depth'=8,'tile'=4] {'depth'}, dimensions={2} | all-to-all | bytes 1048576 | tf_op jit(solution)/shard_map/all_to_all | solution.py:71
  75.1 0.1 copy.9
  75.2 0.1 convert.2
  75.3 0.1 fusion.36
  75.4 0.1 fusion.28
  75.6 0.7 fusion.32
  (11 shorter events, 0.2 us)
Async XLA Ops:
  1.0 6.1 %collective-permute-start = (bf16[1,256,256]{2,1,0:T(8,128)(2,1)S(1)}, bf16[1,256,256]{2,1,0:T(8,128)(2,1)S(1)}, u32[]{:S(2)}, u32[]{:S(2)}) collective-permute-start(bf16[1,256,256]{2,1,0:T(8,128)(2,1)S(1)} %get-tuple-element.180), channel_id=1, source_target_pairs={{0,4},{4,8},{8,12},{12,16},{16,20},{20,24},{24,28},{1,5},{5,9},{9,... | collective-permute-start | bytes 393224 | tf_op jit(solution)/shard_map/ppermute | solution.py:15
  4.9 5.7 %collective-permute-start.1 = (bf16[1,256,256]{2,1,0:T(8,128)(2,1)S(1)}, bf16[1,256,256]{2,1,0:T(8,128)(2,1)S(1)}, u32[]{:S(2)}, u32[]{:S(2)}) collective-permute-start(bf16[1,256,256]{2,1,0:T(8,128)(2,1)S(1)} %get-tuple-element.179), channel_id=1, source_target_pairs={{4,0},{8,4},{12,8},{16,12},{20,16},{24,20},{28,24},{5,1},{9,5},{13... | collective-permute-start | bytes 393224 | tf_op jit(solution)/shard_map/ppermute | solution.py:17
  10.9 9.8 %collective-permute-start.2 = (bf16[6,256,1]{2,1,0:T(8,128)(2,1)S(1)}, bf16[6,256,1]{2,1,0:T(8,128)(2,1)S(1)}, u32[]{:S(2)}, u32[]{:S(2)}) collective-permute-start(bf16[6,256,1]{2,1,0:T(8,128)(2,1)S(1)} %get-tuple-element.175), channel_id=1, source_target_pairs={{0,1},{1,2},{2,3},{4,5},{5,6},{6,7},{8,9},{9,10},{10,11},{12,13},{... | collective-permute-start | bytes 9224 | tf_op jit(solution)/shard_map/ppermute | solution.py:15
  16.0 9.2 %collective-permute-start.3 = (bf16[6,256,1]{2,1,0:T(8,128)(2,1)S(1)}, bf16[6,256,1]{2,1,0:T(8,128)(2,1)}, u32[]{:S(2)}, u32[]{:S(2)}) collective-permute-start(bf16[6,256,1]{2,1,0:T(8,128)(2,1)S(1)} %get-tuple-element.176), channel_id=1, source_target_pairs={{1,0},{2,1},{3,2},{5,4},{6,5},{7,6},{9,8},{10,9},{11,10},{13,12},{... | collective-permute-start | bytes 9224 | tf_op jit(solution)/shard_map/ppermute | solution.py:17
  18.0 9.3 %copy-start = (f32[3,16]{1,0:T(4,128)S(1)}, f32[3,16]{1,0:T(4,128)}, u32[]{:S(2)}) copy-start(f32[3,16]{1,0:T(4,128)} %param.6) | copy-start | bytes 580
  18.0 9.3 %copy-start.1 = (f32[16]{0:T(128)S(1)}, f32[16]{0:T(128)}, u32[]{:S(2)}) copy-start(f32[16]{0:T(128)} %param.7) | copy-start | bytes 196
where the time goes:
time: 76.6 us; the launch traced here: 76.3 us
  matrix products  22.7 us (30%)
  blocking collectives  15.3 us (20%)
  starting transfers between devices  12.3 us (16%)
  other arithmetic  11.6 us (15%)
  waiting for transfers between devices  10.6 us (14%)
  local copies, waits for them, and re-layouts  3.28 us (4%)
    all_to_all x1, blocking collectives, local(): lax.all_to_all(stacked.astype(jnp.bfloat16), 'depth', split_axis=2, conca...  15.3 us
    dot_general x4, matrix products, shade_sample(): jnp.einsum('ck,kxy->cxy', tf_color, weights, precision=lax.Precision.HIGH...  11.7 us
    dot_general x4, matrix products, shade_sample(): jnp.einsum('k,kxy->xy', tf_extinction, weights, precision=lax.Precision.H...  11.1 us
    ppermute x2, starting transfers between devices, extended(): lax.ppermute(tail, axis, [(i, (i + 1) % count) for i in range(ends)])  9.08 us
    ppermute x2, waiting for transfers between devices, extended(): lax.ppermute(head, axis, [((i + 1) % count, i) for i in range(ends)])  6.96 us
    add x7, other arithmetic, composite(): return nearer + (1.0 - nearer[3:4]) * farther  4.08 us
    ppermute x2, waiting for transfers between devices, extended(): lax.ppermute(tail, axis, [(i, (i + 1) % count) for i in range(ends)])  3.59 us
    ppermute x2, starting transfers between devices, extended(): lax.ppermute(head, axis, [((i + 1) % count, i) for i in range(ends)])  3.21 us
  transfers between devices with their start and end apart: 4, of which 4 were waited for; matrix products, arithmetic and copies ran while one was open for 1% of the time, Pallas kernels for 0%

commit v1 on v0

--- a/solution.py
+++ b/solution.py
@@ -1,6 +1,10 @@
+import functools
+
 import jax
 import jax.numpy as jnp
 from jax import lax
+from jax.experimental import pallas as pl
+from jax.experimental.pallas import tpu as pltpu
 from jax.sharding import PartitionSpec as P
 
 
@@ -78,8 +82,346 @@
     return final_image
 
 
+MESH = pl.DeviceIdType.MESH
+LANES = 128
+SUBLANES = 8
+
+
+def iota(shape, dim):
+    return lax.broadcasted_iota(jnp.int32, shape, dim)
+
+
+def stencil(chosen_up, chosen_down):
+    return jnp.where(chosen_up, 0.5, jnp.where(chosen_down, -0.5, 0.0))
+
+
+def render_kernel(
+    depth_count,
+    tile_count,
+    vort_hbm,
+    color_ref,
+    extinction_ref,
+    out_ref,
+    brick,
+    slabs,
+    row_out,
+    row_in,
+    edge_out,
+    edge_in,
+    local_sem,
+    own_sem,
+    send_sem,
+    recv_sem,
+    row_send_sem,
+    row_recv_sem,
+    edge_send_sem,
+    edge_recv_sem,
+):
+    local_slices, tile_rows, tile_cols = vort_hbm.shape
+    rows = tile_rows // depth_count
+    knots = extinction_ref.shape[0]
+    thickness = 1.0 / (local_slices * depth_count)
+    group = local_slices * rows
+    depth = lax.axis_index("depth")
+    tile = lax.axis_index("tile")
+    left = lax.rem(tile + tile_count - 1, tile_count)
+    right = lax.rem(tile + 1, tile_count)
+
+    whole = pltpu.make_async_copy(vort_hbm, brick, local_sem)
+    whole.start()
+
+    def slot(block):
+        return slabs.at[pl.ds(1 + block * local_slices, local_slices)]
+
+    def block_rows(block):
+        return vort_hbm.at[:, pl.ds(pl.multiple_of(block * rows, rows), rows), :]
+
+    own = pltpu.make_async_copy(block_rows(depth), slot(depth), own_sem)
+    own.start()
+
+    barrier = pltpu.get_barrier_semaphore()
+    for step in range(depth_count):
+        peer = lax.rem(depth + step, depth_count)
+        if step > 0:
+            pl.semaphore_signal(barrier, inc=1, device_id=(peer, tile), device_id_type=MESH)
+        for side in (left, right):
+            pl.semaphore_signal(barrier, inc=1, device_id=(peer, side), device_id_type=MESH)
+    pl.semaphore_wait(barrier, 3 * depth_count - 1)
+
+    sends = []
+    for step in range(1, depth_count):
+        peer = lax.rem(depth + step, depth_count)
+        copy = pltpu.make_async_remote_copy(
+            src_ref=block_rows(peer),
+            dst_ref=slot(depth),
+            send_sem=send_sem.at[step],
+            recv_sem=recv_sem.at[depth],
+            device_id=(peer, tile),
+            device_id_type=MESH,
+        )
+        copy.start()
+        sends.append(copy)
+
+    whole.wait()
+    packed = depth_count * 2 * local_slices
+    line = iota((packed, 1), 0)
+    line_block = line // (2 * local_slices)
+    line_slice = (line % (2 * local_slices)) // 2
+    line_row = line_block * rows + jnp.where(line % 2 == 0, -1, rows)
+    inside = (line_row >= 0) & (line_row < tile_rows)
+    wanted = jnp.where(inside, line_slice * tile_rows + line_row, -1)
+    pick = jnp.where(iota((packed, local_slices * tile_rows), 1) == wanted, 1.0, 0.0)
+    flat = brick[...].reshape(local_slices * tile_rows, tile_cols)
+    outside = jnp.dot(pick.astype(jnp.bfloat16), flat, preferred_element_type=jnp.float32)
+    for block in range(depth_count):
+        first = block * 2 * local_slices
+        row_out[block] = outside[first : first + 2 * local_slices].astype(jnp.bfloat16)
+    column = iota((SUBLANES, tile_cols), 1)
+    ends = iota((SUBLANES, tile_cols), 0)
+    pick_ends = ((ends == 0) & (column == 0)) | ((ends == 1) & (column == tile_cols - 1))
+    by_block = jnp.concatenate(
+        [
+            brick[z, block * rows : (block + 1) * rows, :]
+            for block in range(depth_count)
+            for z in range(local_slices)
+        ],
+        axis=0,
+    )
+    columns = lax.dot_general(
+        jnp.where(pick_ends, 1.0, 0.0).astype(jnp.bfloat16),
+        by_block,
+        (((1,), (1,)), ((), ())),
+        preferred_element_type=jnp.float32,
+    )
+    for block in range(depth_count):
+        for end in range(2):
+            edge_out[end, block] = columns[end : end + 1, block * group : (block + 1) * group]
+
+    row_in[depth] = row_out[depth]
+    for step in range(depth_count):
+        peer = lax.rem(depth + step, depth_count)
+        if step > 0:
+            copy = pltpu.make_async_remote_copy(
+                src_ref=row_out.at[peer],
+                dst_ref=row_in.at[depth],
+                send_sem=row_send_sem.at[step],
+                recv_sem=row_recv_sem.at[depth],
+                device_id=(peer, tile),
+                device_id_type=MESH,
+            )
+            copy.start()
+            sends.append(copy)
+        for end, beside in enumerate((left, right)):
+            copy = pltpu.make_async_remote_copy(
+                src_ref=edge_out.at[end, peer],
+                dst_ref=edge_in.at[1 - end, depth],
+                send_sem=edge_send_sem.at[end, step],
+                recv_sem=edge_recv_sem.at[1 - end, depth],
+                device_id=(peer, beside),
+                device_id_type=MESH,
+            )
+            copy.start()
+            sends.append(copy)
+
+    blank = jnp.zeros((1, rows, tile_cols), jnp.bfloat16)
+    slabs[0:1] = blank
+    slabs[1 + depth_count * local_slices : 2 + depth_count * local_slices] = blank
+
+    spread = (2 + local_slices) * rows
+    extra = 2 * SUBLANES
+    cell = iota((group, spread + extra), 0)
+    source = iota((group, spread + extra), 1)
+    cell_row = cell % rows
+    in_slabs = source < spread
+    up = in_slabs & (source == cell + rows + 1) & (cell_row < rows - 1)
+    down = in_slabs & (source == cell + rows - 1) & (cell_row > 0)
+    packed_line = spread + 2 * (cell // rows)
+    up = up | ((source == packed_line + 1) & (cell_row == rows - 1))
+    down = down | ((source == packed_line) & (cell_row == 0))
+    along_x = stencil(up, down).astype(jnp.bfloat16)
+    along_z = stencil(in_slabs & (source == cell + 2 * rows), in_slabs & (source == cell)).astype(jnp.bfloat16)
+    to_col = iota((tile_cols, tile_cols), 1)
+    from_col = iota((tile_cols, tile_cols), 0)
+    along_y = stencil(from_col == to_col + 1, from_col == to_col - 1).astype(jnp.bfloat16)
+    has_left = jnp.where(tile > 0, -0.5, 0.0)
+    has_right = jnp.where(tile < tile_count - 1, 0.5, 0.0)
+    place = jnp.where(
+        (ends == 0) & (column == 0),
+        has_left,
+        jnp.where((ends == 1) & (column == tile_cols - 1), has_right, 0.0),
+    ).astype(jnp.bfloat16)
+
+    lane = iota((rows, LANES), 1)
+
+    def table(read):
+        value = jnp.zeros((rows, LANES), jnp.float32)
+        for k in range(knots):
+            value = jnp.where(lane == k, read(k), value)
+        slope = jnp.zeros((rows, LANES), jnp.float32)
+        for k in range(knots - 1):
+            slope = jnp.where(lane == k, read(k + 1) - read(k), slope)
+        return value, slope
+
+    tables = [table(lambda k, c=c: color_ref[c, k]) for c in range(3)]
+    tables.append(table(lambda k: -thickness * extinction_ref[k]))
+
+    def lookup(which, index, part):
+        value, slope = tables[which]
+        pieces = []
+        for first in range(0, tile_cols, LANES):
+            at = index[:, first : first + LANES]
+            base = jnp.take_along_axis(value, at, axis=1, mode="promise_in_bounds")
+            rise = jnp.take_along_axis(slope, at, axis=1, mode="promise_in_bounds")
+            pieces.append(base + part[:, first : first + LANES] * rise)
+        return jnp.concatenate(pieces, axis=1)
+
+    own.wait()
+    forward = depth < depth_count // 2
+
+    def wait_recv(dst, sem):
+        pltpu.make_async_remote_copy(
+            src_ref=dst,
+            dst_ref=dst,
+            send_sem=send_sem.at[0],
+            recv_sem=sem,
+            device_id=(depth, tile),
+            device_id_type=MESH,
+        ).wait_recv()
+
+    def wait_block(block):
+        @pl.when(block != depth)
+        def _():
+            wait_recv(slot(block), recv_sem.at[block])
+
+    def over(near, far):
+        clear = 1.0 - near[3]
+        return tuple(n + clear * f for n, f in zip(near, far))
+
+    def order(step):
+        return jnp.where(forward, step, depth_count - 1 - step)
+
+    wait_block(order(0))
+
+    def march(step, total):
+        block = order(step)
+
+        @pl.when(step < depth_count - 1)
+        def _():
+            wait_block(order(step + 1))
+
+        @pl.when(block != depth)
+        def _():
+            wait_recv(row_in.at[block], row_recv_sem.at[block])
+
+        wait_recv(edge_in.at[0, block], edge_recv_sem.at[0, block])
+        wait_recv(edge_in.at[1, block], edge_recv_sem.at[1, block])
+
+        around = slabs[pl.ds(block * local_slices, local_slices + 2)].reshape(spread, tile_cols)
+        lines = row_in[block].astype(jnp.float32)
+        lines = jnp.concatenate(
+            [lines, jnp.zeros((extra - 2 * local_slices, tile_cols), jnp.float32)], axis=0
+        ).astype(jnp.bfloat16)
+        around = jnp.concatenate([around, lines], axis=0)
+        grads_x = jnp.dot(along_x, around, preferred_element_type=jnp.float32)
+        grads_z = jnp.dot(along_z, around, preferred_element_type=jnp.float32)
+        cells = slabs[pl.ds(1 + block * local_slices, local_slices)].reshape(group, tile_cols)
+        edge_row = iota((SUBLANES, group), 0)
+        edges = jnp.where(
+            edge_row == 0, edge_in[0, block], jnp.where(edge_row == 1, edge_in[1, block], 0.0)
+        )
+        grads_y = jnp.dot(cells, along_y, preferred_element_type=jnp.float32) + lax.dot_general(
+            edges.astype(jnp.bfloat16),
+            place,
+            (((0,), (0,)), ((), ())),
+            preferred_element_type=jnp.float32,
+        )
+        partial = None
+        for z in range(local_slices):
+            here = slice(z * rows, (z + 1) * rows)
+            gx, gy, gz = grads_x[here], grads_y[here], grads_z[here]
+            scalar = cells[here].astype(jnp.float32)
+            facing = 0.48 * gx + 0.6 * gy + 0.64 * gz
+            lighting = 0.55 + 0.45 * facing * lax.rsqrt(gx * gx + gy * gy + gz * gz + 0.25)
+            position = jnp.clip((scalar + 4.0) * ((knots - 1) / 8.0), 0.0, knots - 1.0)
+            index = position.astype(jnp.int32)
+            part = position - index.astype(jnp.float32)
+            opacity = 1.0 - jnp.exp(lookup(3, index, part))
+            lit = opacity * lighting
+            sample = tuple(lit * lookup(c, index, part) for c in range(3)) + (opacity,)
+            partial = sample if partial is None else over(partial, sample)
+        near = tuple(jnp.where(forward, t, p) for t, p in zip(total, partial))
+        far = tuple(jnp.where(forward, p, t) for t, p in zip(total, partial))
+        return over(near, far)
+
+    nothing = tuple(jnp.zeros((rows, tile_cols), jnp.float32) for _ in range(4))
+    total = lax.fori_loop(0, depth_count, march, nothing)
+    for channel in range(4):
+        out_ref[channel] = total[channel]
+    for copy in sends:
+        copy.wait_send()
+
+
+def render(vorticity, tf_color, tf_extinction):
+    depth_count = lax.axis_size("depth")
+    tile_count = lax.axis_size("tile")
+    local_slices, tile_rows, tile_cols = vorticity.shape
+    rows = tile_rows // depth_count
+    group = local_slices * rows
+    dma = pltpu.SemaphoreType.DMA
+    return pl.pallas_call(
+        functools.partial(render_kernel, depth_count, tile_count),
+        out_shape=jax.ShapeDtypeStruct((4, rows, tile_cols), jnp.float32),
+        in_specs=[
+            pl.BlockSpec(memory_space=pl.ANY),
+            pl.BlockSpec(memory_space=pltpu.SMEM),
+            pl.BlockSpec(memory_space=pltpu.SMEM),
+        ],
+        out_specs=pl.BlockSpec(memory_space=pltpu.VMEM),
+        scratch_shapes=[
+            pltpu.VMEM((local_slices, tile_rows, tile_cols), jnp.bfloat16),
+            pltpu.VMEM((depth_count * local_slices + 2, rows, tile_cols), jnp.bfloat16),
+            pltpu.VMEM((depth_count, 2 * local_slices, tile_cols), jnp.bfloat16),
+            pltpu.VMEM((depth_count, 2 * local_slices, tile_cols), jnp.bfloat16),
+            pltpu.VMEM((2, depth_count, 1, group), jnp.float32),
+            pltpu.VMEM((2, depth_count, 1, group), jnp.float32),
+            dma,
+            dma,
+            dma((depth_count,)),
+            dma((depth_count,)),
+            dma((depth_count,)),
+            dma((depth_count,)),
+            dma((2, depth_count)),
+            dma((2, depth_count)),
+        ],
+        compiler_params=pltpu.CompilerParams(collective_id=0, has_side_effects=True),
+        name="render",
+    )(vorticity, tf_color, tf_extinction)
+
+
+def fits(vorticity, knots):
+    local_slices, tile_rows, tile_cols = vorticity.shape
+    depth_count = lax.axis_size("depth")
+    rows = tile_rows // depth_count
+    return (
+        tile_rows % depth_count == 0
+        and rows % (2 * SUBLANES) == 0
+        and tile_cols % LANES == 0
+        and (local_slices * rows) % LANES == 0
+        and 2 * local_slices == SUBLANES
+        and knots <= LANES
+        and depth_count <= 16
+        and lax.axis_size("tile") > 1
+    )
+
+
+def choose(vorticity, tf_color, tf_extinction):
+    if fits(vorticity, tf_extinction.shape[0]):
+        return render(vorticity, tf_color, tf_extinction)
+    return local(vorticity, tf_color, tf_extinction)
+
+
 def solution(mesh):
     placed = (P("depth", None, "tile"), P(), P())
     return jax.shard_map(
-        local, mesh=mesh, in_specs=placed, out_specs=P(None, "depth", "tile"), check_vma=False
-    )
+        choose, mesh=mesh, in_specs=placed, out_specs=P(None, "depth", "tile"), check_vma=False
+    )

time: 76.6 us -> 27.9 us (0.36)
  the two profiles are of different devices: /device:TPU:1 before, /device:TPU:0 now
where the time goes in v1:
time: 27.9 us; the launch traced here: 27.7 us
  Pallas kernels  26.2 us (94%)
  local copies, waits for them, and re-layouts  1.57 us (6%)
    pallas_call x1, Pallas kernels, render(): pl.pallas_call(functools.partial(render_kernel, depth_count, tile_count),...  26.2 us
    unnamed x1, local copies, waits for them, and re-layouts  1.57 us

profile of v1, /device:TPU:0, one launch (start us, length us, event | category | flops | bytes accessed | tf_op | source)
XLA Modules:
  0.0 27.7 jit_solution(2251473742022164541)
XLA Ops:
  0.0 26.2 %render.1 = f32[4,32,256]{2,1,0:T(8,128)} custom-call(bf16[4,256,256]{2,1,0:T(8,128)(2,1)} %vort_hbm.1, f32[3,16]{1,0:T(4,128)} %color_ref.1, f32[16]{0:T(128)} %extinction_ref.1), custom_call_target="tpu_custom_call" | custom-call | tf_op jit(solution)/shard_map/render/pallas_call | solution.py:371
  26.2 1.6 %copy.5 = f32[4,32,256]{2,1,0:T(8,128)} copy(f32[4,32,256]{2,1,0:T(8,128)} %render.1) | data formatting | bytes 262144

commit v2 on v1

--- a/solution.py
+++ b/solution.py
@@ -84,6 +84,7 @@
 
 MESH = pl.DeviceIdType.MESH
 LANES = 128
+PAIR = 2
 SUBLANES = 8
 
 
@@ -108,6 +109,9 @@
     row_in,
     edge_out,
     edge_in,
+    part_out,
+    part_in,
+    part_own,
     local_sem,
     own_sem,
     send_sem,
@@ -116,51 +120,107 @@
     row_recv_sem,
     edge_send_sem,
     edge_recv_sem,
+    halo_send_sem,
+    halo_recv_sem,
+    part_send_sem,
+    part_recv_sem,
 ):
-    local_slices, tile_rows, tile_cols = vort_hbm.shape
-    rows = tile_rows // depth_count
+    local_slices, pairs, _, rows, tile_cols = vort_hbm.shape
+    tile_rows = depth_count * rows
     knots = extinction_ref.shape[0]
     thickness = 1.0 / (local_slices * depth_count)
     group = local_slices * rows
+    pair_slices = PAIR * local_slices
     depth = lax.axis_index("depth")
     tile = lax.axis_index("tile")
+    pair = depth // PAIR
+    member = depth % PAIR
+    mate = 1 - member
     left = lax.rem(tile + tile_count - 1, tile_count)
     right = lax.rem(tile + 1, tile_count)
 
     whole = pltpu.make_async_copy(vort_hbm, brick, local_sem)
     whole.start()
 
-    def slot(block):
-        return slabs.at[pl.ds(1 + block * local_slices, local_slices)]
-
-    def block_rows(block):
-        return vort_hbm.at[:, pl.ds(pl.multiple_of(block * rows, rows), rows), :]
-
-    own = pltpu.make_async_copy(block_rows(depth), slot(depth), own_sem)
-    own.start()
+    def slot(chunk, which):
+        return slabs.at[chunk, pl.ds(1 + which * local_slices, local_slices)]
+
+    own = [
+        pltpu.make_async_copy(vort_hbm.at[:, chunk, member], slot(chunk, member), own_sem.at[chunk])
+        for chunk in range(pairs)
+    ]
+    for copy in own:
+        copy.start()
 
     barrier = pltpu.get_barrier_semaphore()
-    for step in range(depth_count):
-        peer = lax.rem(depth + step, depth_count)
-        if step > 0:
-            pl.semaphore_signal(barrier, inc=1, device_id=(peer, tile), device_id_type=MESH)
-        for side in (left, right):
-            pl.semaphore_signal(barrier, inc=1, device_id=(peer, side), device_id_type=MESH)
-    pl.semaphore_wait(barrier, 3 * depth_count - 1)
-
-    sends = []
     for step in range(1, depth_count):
         peer = lax.rem(depth + step, depth_count)
-        copy = pltpu.make_async_remote_copy(
-            src_ref=block_rows(peer),
-            dst_ref=slot(depth),
-            send_sem=send_sem.at[step],
-            recv_sem=recv_sem.at[depth],
-            device_id=(peer, tile),
+        pl.semaphore_signal(barrier, inc=1, device_id=(peer, tile), device_id_type=MESH)
+    for which in range(PAIR):
+        for side in (left, right):
+            pl.semaphore_signal(
+                barrier, inc=1, device_id=(pair * PAIR + which, side), device_id_type=MESH
+            )
+    pl.semaphore_wait(barrier, depth_count - 1 + 2 * PAIR)
+
+    def remote(src, dst, sent, received, target):
+        return pltpu.make_async_remote_copy(
+            src_ref=src,
+            dst_ref=dst,
+            send_sem=sent,
+            recv_sem=received,
+            device_id=target,
             device_id_type=MESH,
+        )
+
+    def order(step):
+        return pair ^ (pairs - 1 - step)
+
+    sends = []
+    for step in range(pairs):
+        chunk = order(step)
+        copy = remote(
+            vort_hbm.at[:, chunk, mate],
+            slot(chunk, member),
+            send_sem.at[step],
+            recv_sem.at[chunk],
+            (pair * PAIR + mate, tile),
         )
         copy.start()
         sends.append(copy)
+
+    def halo(which, beyond):
+        at = PAIR * local_slices + 1 if beyond < 0 else 0
+        return remote(
+            vort_hbm.at[0 if beyond < 0 else local_slices - 1, :, which],
+            slabs.at[:, at],
+            halo_send_sem.at[which],
+            halo_recv_sem.at[0 if beyond > 0 else 1],
+            ((pair + beyond) * PAIR + which, tile),
+        )
+
+    to_below = (member == 0) & (pair > 0)
+    to_above = (member == PAIR - 1) & (pair < pairs - 1)
+
+    @pl.when(to_below)
+    def _():
+        for which in range(PAIR):
+            halo(which, -1).start()
+
+    @pl.when(to_above)
+    def _():
+        for which in range(PAIR):
+            halo(which, 1).start()
+
+    blank = jnp.zeros((pairs, 1, rows, tile_cols), jnp.bfloat16)
+
+    @pl.when(pair == 0)
+    def _():
+        slabs[:, 0:1] = blank
+
+    @pl.when(pair == pairs - 1)
+    def _():
+        slabs[:, pair_slices + 1 : pair_slices + 2] = blank
 
     whole.wait()
     packed = depth_count * 2 * local_slices
@@ -175,13 +235,13 @@
     outside = jnp.dot(pick.astype(jnp.bfloat16), flat, preferred_element_type=jnp.float32)
     for block in range(depth_count):
         first = block * 2 * local_slices
-        row_out[block] = outside[first : first + 2 * local_slices].astype(jnp.bfloat16)
+        row_out[block % PAIR, block // PAIR] = outside[first : first + 2 * local_slices].astype(jnp.bfloat16)
     column = iota((SUBLANES, tile_cols), 1)
     ends = iota((SUBLANES, tile_cols), 0)
     pick_ends = ((ends == 0) & (column == 0)) | ((ends == 1) & (column == tile_cols - 1))
     by_block = jnp.concatenate(
         [
-            brick[z, block * rows : (block + 1) * rows, :]
+            brick[z, block // PAIR, block % PAIR]
             for block in range(depth_count)
             for z in range(local_slices)
         ],
@@ -195,37 +255,29 @@
     )
     for block in range(depth_count):
         for end in range(2):
-            edge_out[end, block] = columns[end : end + 1, block * group : (block + 1) * group]
-
-    row_in[depth] = row_out[depth]
-    for step in range(depth_count):
-        peer = lax.rem(depth + step, depth_count)
-        if step > 0:
-            copy = pltpu.make_async_remote_copy(
-                src_ref=row_out.at[peer],
-                dst_ref=row_in.at[depth],
-                send_sem=row_send_sem.at[step],
-                recv_sem=row_recv_sem.at[depth],
-                device_id=(peer, tile),
-                device_id_type=MESH,
+            edge_out[end, block % PAIR, block // PAIR] = columns[end : end + 1, block * group : (block + 1) * group]
+
+    row_in[member] = row_out[member]
+    copy = remote(
+        row_out.at[mate],
+        row_in.at[member],
+        row_send_sem,
+        row_recv_sem,
+        (pair * PAIR + mate, tile),
+    )
+    copy.start()
+    sends.append(copy)
+    for which in range(PAIR):
+        for end, beside in enumerate((left, right)):
+            copy = remote(
+                edge_out.at[end, which],
+                edge_in.at[1 - end, member],
+                edge_send_sem.at[end, which],
+                edge_recv_sem.at[1 - end, member],
+                (pair * PAIR + which, beside),
             )
             copy.start()
             sends.append(copy)
-        for end, beside in enumerate((left, right)):
-            copy = pltpu.make_async_remote_copy(
-                src_ref=edge_out.at[end, peer],
-                dst_ref=edge_in.at[1 - end, depth],
-                send_sem=edge_send_sem.at[end, step],
-                recv_sem=edge_recv_sem.at[1 - end, depth],
-                device_id=(peer, beside),
-                device_id_type=MESH,
-            )
-            copy.start()
-            sends.append(copy)
-
-    blank = jnp.zeros((1, rows, tile_cols), jnp.bfloat16)
-    slabs[0:1] = blank
-    slabs[1 + depth_count * local_slices : 2 + depth_count * local_slices] = blank
 
     spread = (2 + local_slices) * rows
     extra = 2 * SUBLANES
@@ -275,59 +327,42 @@
             pieces.append(base + part[:, first : first + LANES] * rise)
         return jnp.concatenate(pieces, axis=1)
 
-    own.wait()
-    forward = depth < depth_count // 2
-
     def wait_recv(dst, sem):
-        pltpu.make_async_remote_copy(
-            src_ref=dst,
-            dst_ref=dst,
-            send_sem=send_sem.at[0],
-            recv_sem=sem,
-            device_id=(depth, tile),
-            device_id_type=MESH,
-        ).wait_recv()
-
-    def wait_block(block):
-        @pl.when(block != depth)
-        def _():
-            wait_recv(slot(block), recv_sem.at[block])
+        remote(dst, dst, row_send_sem, sem, (depth, tile)).wait_recv()
+
+    for copy in own:
+        copy.wait()
+
+    @pl.when(pair > 0)
+    def _():
+        wait_recv(slabs.at[:, 0], halo_recv_sem.at[0])
+
+    @pl.when(pair < pairs - 1)
+    def _():
+        wait_recv(slabs.at[:, pair_slices + 1], halo_recv_sem.at[1])
+
+    wait_recv(row_in.at[mate], row_recv_sem)
+    for end in range(2):
+        for which in range(PAIR):
+            wait_recv(edge_in.at[end, which], edge_recv_sem.at[end, which])
 
     def over(near, far):
         clear = 1.0 - near[3]
         return tuple(n + clear * f for n, f in zip(near, far))
 
-    def order(step):
-        return jnp.where(forward, step, depth_count - 1 - step)
-
-    wait_block(order(0))
-
-    def march(step, total):
-        block = order(step)
-
-        @pl.when(step < depth_count - 1)
-        def _():
-            wait_block(order(step + 1))
-
-        @pl.when(block != depth)
-        def _():
-            wait_recv(row_in.at[block], row_recv_sem.at[block])
-
-        wait_recv(edge_in.at[0, block], edge_recv_sem.at[0, block])
-        wait_recv(edge_in.at[1, block], edge_recv_sem.at[1, block])
-
-        around = slabs[pl.ds(block * local_slices, local_slices + 2)].reshape(spread, tile_cols)
-        lines = row_in[block].astype(jnp.float32)
+    def shade(chunk, which, partial):
+        around = slabs[chunk, which * local_slices : (which + 1) * local_slices + 2].reshape(spread, tile_cols)
+        lines = row_in[which, chunk].astype(jnp.float32)
         lines = jnp.concatenate(
             [lines, jnp.zeros((extra - 2 * local_slices, tile_cols), jnp.float32)], axis=0
         ).astype(jnp.bfloat16)
         around = jnp.concatenate([around, lines], axis=0)
         grads_x = jnp.dot(along_x, around, preferred_element_type=jnp.float32)
         grads_z = jnp.dot(along_z, around, preferred_element_type=jnp.float32)
-        cells = slabs[pl.ds(1 + block * local_slices, local_slices)].reshape(group, tile_cols)
+        cells = slabs[chunk, 1 + which * local_slices : 1 + (which + 1) * local_slices].reshape(group, tile_cols)
         edge_row = iota((SUBLANES, group), 0)
         edges = jnp.where(
-            edge_row == 0, edge_in[0, block], jnp.where(edge_row == 1, edge_in[1, block], 0.0)
+            edge_row == 0, edge_in[0, which, chunk], jnp.where(edge_row == 1, edge_in[1, which, chunk], 0.0)
         )
         grads_y = jnp.dot(cells, along_y, preferred_element_type=jnp.float32) + lax.dot_general(
             edges.astype(jnp.bfloat16),
@@ -335,7 +370,6 @@
             (((0,), (0,)), ((), ())),
             preferred_element_type=jnp.float32,
         )
-        partial = None
         for z in range(local_slices):
             here = slice(z * rows, (z + 1) * rows)
             gx, gy, gz = grads_x[here], grads_y[here], grads_z[here]
@@ -349,16 +383,61 @@
             lit = opacity * lighting
             sample = tuple(lit * lookup(c, index, part) for c in range(3)) + (opacity,)
             partial = sample if partial is None else over(partial, sample)
-        near = tuple(jnp.where(forward, t, p) for t, p in zip(total, partial))
-        far = tuple(jnp.where(forward, p, t) for t, p in zip(total, partial))
-        return over(near, far)
-
-    nothing = tuple(jnp.zeros((rows, tile_cols), jnp.float32) for _ in range(4))
-    total = lax.fori_loop(0, depth_count, march, nothing)
+        return partial
+
+    def send_part(step):
+        chunk = order(step)
+        return remote(
+            part_out.at[chunk],
+            part_in.at[pair],
+            part_send_sem.at[chunk],
+            part_recv_sem.at[pair],
+            (chunk * PAIR + member, tile),
+        )
+
+    def march(step, carry):
+        chunk = order(step)
+        wait_recv(slot(chunk, mate), recv_sem.at[chunk])
+        partial = None
+        for which in range(PAIR):
+            partial = shade(chunk, which, partial)
+        for channel in range(4):
+            part_own[channel] = partial[channel]
+            part_out[chunk, channel] = partial[channel].astype(jnp.bfloat16)
+
+        @pl.when(step < pairs - 1)
+        def _():
+            send_part(step).start()
+
+        return carry
+
+    lax.fori_loop(0, pairs, march, 0)
+    part_in[pair] = part_out[pair]
+    for step in range(pairs - 1):
+        wait_recv(part_in.at[order(step)], part_recv_sem.at[order(step)])
+    total = None
+    for source in range(pairs):
+        layer = tuple(
+            jnp.where(pair == source, part_own[c], part_in[source, c].astype(jnp.float32))
+            for c in range(4)
+        )
+        total = layer if total is None else over(total, layer)
     for channel in range(4):
         out_ref[channel] = total[channel]
     for copy in sends:
         copy.wait_send()
+    for step in range(pairs - 1):
+        send_part(step).wait_send()
+
+    @pl.when(to_below)
+    def _():
+        for which in range(PAIR):
+            halo(which, -1).wait_send()
+
+    @pl.when(to_above)
+    def _():
+        for which in range(PAIR):
+            halo(which, 1).wait_send()
 
 
 def render(vorticity, tf_color, tf_extinction):
@@ -367,6 +446,7 @@
     local_slices, tile_rows, tile_cols = vorticity.shape
     rows = tile_rows // depth_count
     group = local_slices * rows
+    pairs = depth_count // PAIR
     dma = pltpu.SemaphoreType.DMA
     return pl.pallas_call(
         functools.partial(render_kernel, depth_count, tile_count),
@@ -378,24 +458,31 @@
         ],
         out_specs=pl.BlockSpec(memory_space=pltpu.VMEM),
         scratch_shapes=[
-            pltpu.VMEM((local_slices, tile_rows, tile_cols), jnp.bfloat16),
-            pltpu.VMEM((depth_count * local_slices + 2, rows, tile_cols), jnp.bfloat16),
-            pltpu.VMEM((depth_count, 2 * local_slices, tile_cols), jnp.bfloat16),
-            pltpu.VMEM((depth_count, 2 * local_slices, tile_cols), jnp.bfloat16),
-            pltpu.VMEM((2, depth_count, 1, group), jnp.float32),
-            pltpu.VMEM((2, depth_count, 1, group), jnp.float32),
+            pltpu.VMEM((local_slices, pairs, PAIR, rows, tile_cols), jnp.bfloat16),
+            pltpu.VMEM((pairs, PAIR * local_slices + 2, rows, tile_cols), jnp.bfloat16),
+            pltpu.VMEM((PAIR, pairs, 2 * local_slices, tile_cols), jnp.bfloat16),
+            pltpu.VMEM((PAIR, pairs, 2 * local_slices, tile_cols), jnp.bfloat16),
+            pltpu.VMEM((2, PAIR, pairs, 1, group), jnp.float32),
+            pltpu.VMEM((2, PAIR, pairs, 1, group), jnp.float32),
+            pltpu.VMEM((pairs, 4, rows, tile_cols), jnp.bfloat16),
+            pltpu.VMEM((pairs, 4, rows, tile_cols), jnp.bfloat16),
+            pltpu.VMEM((4, rows, tile_cols), jnp.float32),
+            dma,
+            dma((pairs,)),
+            dma((pairs,)),
+            dma((pairs,)),
             dma,
             dma,
-            dma((depth_count,)),
-            dma((depth_count,)),
-            dma((depth_count,)),
-            dma((depth_count,)),
-            dma((2, depth_count)),
-            dma((2, depth_count)),
+            dma((2, PAIR)),
+            dma((2, PAIR)),
+            dma((PAIR,)),
+            dma((2,)),
+            dma((pairs,)),
+            dma((pairs,)),
         ],
         compiler_params=pltpu.CompilerParams(collective_id=0, has_side_effects=True),
         name="render",
-    )(vorticity, tf_color, tf_extinction)
+    )(vorticity.reshape(local_slices, pairs, PAIR, rows, tile_cols), tf_color, tf_extinction)
 
 
 def fits(vorticity, knots):
@@ -409,6 +496,8 @@
         and (local_slices * rows) % LANES == 0
         and 2 * local_slices == SUBLANES
         and knots <= LANES
+        and depth_count % PAIR == 0
+        and depth_count & (depth_count - 1) == 0
         and depth_count <= 16
         and lax.axis_size("tile") > 1
     )

time: 27.9 us -> 27.6 us (0.989)
  Pallas kernels: 26.2 us -> 25.9 us
where the time goes in v2:
time: 27.6 us; the launch traced here: 27.5 us
  Pallas kernels  25.9 us (94%)
  local copies, waits for them, and re-layouts  1.57 us (6%)
    pallas_call x1, Pallas kernels, render(): pl.pallas_call(functools.partial(render_kernel, depth_count, tile_count),...  25.9 us
    unnamed x1, local copies, waits for them, and re-layouts  1.57 us

profile of v2, /device:TPU:0, one launch (start us, length us, event | category | flops | bytes accessed | tf_op | source)
XLA Modules:
  0.0 27.5 jit_solution(18164543162158369259)
XLA Ops:
  0.0 25.9 %render.1 = f32[4,32,256]{2,1,0:T(8,128)} custom-call(bf16[4,4,2,32,256]{4,3,2,1,0:T(8,128)(2,1)} %bitcast.1, f32[3,16]{1,0:T(4,128)} %color_ref.1, f32[16]{0:T(128)} %extinction_ref.1), custom_call_target="tpu_custom_call" | custom-call | tf_op jit(solution)/shard_map/render/pallas_call | solution.py:451
  25.9 1.6 %copy.5 = f32[4,32,256]{2,1,0:T(8,128)} copy(f32[4,32,256]{2,1,0:T(8,128)} %render.1) | data formatting | bytes 262144

commit v3 on v2

--- a/solution.py
+++ b/solution.py
@@ -161,67 +161,6 @@
             pl.semaphore_signal(
                 barrier, inc=1, device_id=(pair * PAIR + which, side), device_id_type=MESH
             )
-    pl.semaphore_wait(barrier, depth_count - 1 + 2 * PAIR)
-
-    def remote(src, dst, sent, received, target):
-        return pltpu.make_async_remote_copy(
-            src_ref=src,
-            dst_ref=dst,
-            send_sem=sent,
-            recv_sem=received,
-            device_id=target,
-            device_id_type=MESH,
-        )
-
-    def order(step):
-        return pair ^ (pairs - 1 - step)
-
-    sends = []
-    for step in range(pairs):
-        chunk = order(step)
-        copy = remote(
-            vort_hbm.at[:, chunk, mate],
-            slot(chunk, member),
-            send_sem.at[step],
-            recv_sem.at[chunk],
-            (pair * PAIR + mate, tile),
-        )
-        copy.start()
-        sends.append(copy)
-
-    def halo(which, beyond):
-        at = PAIR * local_slices + 1 if beyond < 0 else 0
-        return remote(
-            vort_hbm.at[0 if beyond < 0 else local_slices - 1, :, which],
-            slabs.at[:, at],
-            halo_send_sem.at[which],
-            halo_recv_sem.at[0 if beyond > 0 else 1],
-            ((pair + beyond) * PAIR + which, tile),
-        )
-
-    to_below = (member == 0) & (pair > 0)
-    to_above = (member == PAIR - 1) & (pair < pairs - 1)
-
-    @pl.when(to_below)
-    def _():
-        for which in range(PAIR):
-            halo(which, -1).start()
-
-    @pl.when(to_above)
-    def _():
-        for which in range(PAIR):
-            halo(which, 1).start()
-
-    blank = jnp.zeros((pairs, 1, rows, tile_cols), jnp.bfloat16)
-
-    @pl.when(pair == 0)
-    def _():
-        slabs[:, 0:1] = blank
-
-    @pl.when(pair == pairs - 1)
-    def _():
-        slabs[:, pair_slices + 1 : pair_slices + 2] = blank
-
     whole.wait()
     packed = depth_count * 2 * local_slices
     line = iota((packed, 1), 0)
@@ -257,28 +196,6 @@
         for end in range(2):
             edge_out[end, block % PAIR, block // PAIR] = columns[end : end + 1, block * group : (block + 1) * group]
 
-    row_in[member] = row_out[member]
-    copy = remote(
-        row_out.at[mate],
-        row_in.at[member],
-        row_send_sem,
-        row_recv_sem,
-        (pair * PAIR + mate, tile),
-    )
-    copy.start()
-    sends.append(copy)
-    for which in range(PAIR):
-        for end, beside in enumerate((left, right)):
-            copy = remote(
-                edge_out.at[end, which],
-                edge_in.at[1 - end, member],
-                edge_send_sem.at[end, which],
-                edge_recv_sem.at[1 - end, member],
-                (pair * PAIR + which, beside),
-            )
-            copy.start()
-            sends.append(copy)
-
     spread = (2 + local_slices) * rows
     extra = 2 * SUBLANES
     cell = iota((group, spread + extra), 0)
@@ -326,6 +243,89 @@
             rise = jnp.take_along_axis(slope, at, axis=1, mode="promise_in_bounds")
             pieces.append(base + part[:, first : first + LANES] * rise)
         return jnp.concatenate(pieces, axis=1)
+
+    blank = jnp.zeros((pairs, 1, rows, tile_cols), jnp.bfloat16)
+
+    @pl.when(pair == 0)
+    def _():
+        slabs[:, 0:1] = blank
+
+    @pl.when(pair == pairs - 1)
+    def _():
+        slabs[:, pair_slices + 1 : pair_slices + 2] = blank
+
+    pl.semaphore_wait(barrier, depth_count - 1 + 2 * PAIR)
+
+    def remote(src, dst, sent, received, target):
+        return pltpu.make_async_remote_copy(
+            src_ref=src,
+            dst_ref=dst,
+            send_sem=sent,
+            recv_sem=received,
+            device_id=target,
+            device_id_type=MESH,
+        )
+
+    def order(step):
+        return pair ^ (pairs - 1 - step)
+
+    sends = []
+    row_in[member] = row_out[member]
+    copy = remote(
+        row_out.at[mate],
+        row_in.at[member],
+        row_send_sem,
+        row_recv_sem,
+        (pair * PAIR + mate, tile),
+    )
+    copy.start()
+    sends.append(copy)
+    for which in range(PAIR):
+        for end, beside in enumerate((left, right)):
+            copy = remote(
+                edge_out.at[end, which],
+                edge_in.at[1 - end, member],
+                edge_send_sem.at[end, which],
+                edge_recv_sem.at[1 - end, member],
+                (pair * PAIR + which, beside),
+            )
+            copy.start()
+            sends.append(copy)
+
+    def halo(which, beyond):
+        at = PAIR * local_slices + 1 if beyond < 0 else 0
+        return remote(
+            vort_hbm.at[0 if beyond < 0 else local_slices - 1, :, which],
+            slabs.at[:, at],
+            halo_send_sem.at[which],
+            halo_recv_sem.at[0 if beyond > 0 else 1],
+            ((pair + beyond) * PAIR + which, tile),
+        )
+
+    to_below = (member == 0) & (pair > 0)
+    to_above = (member == PAIR - 1) & (pair < pairs - 1)
+
+    @pl.when(to_below)
+    def _():
+        for which in range(PAIR):
+            halo(which, -1).start()
+
+    @pl.when(to_above)
+    def _():
+        for which in range(PAIR):
+            halo(which, 1).start()
+
+    for step in range(pairs):
+        chunk = order(step)
+        copy = remote(
+            vort_hbm.at[:, chunk, mate],
+            slot(chunk, member),
+            send_sem.at[step],
+            recv_sem.at[chunk],
+            (pair * PAIR + mate, tile),
+        )
+        copy.start()
+        sends.append(copy)
 
     def wait_recv(dst, sem):
         remote(dst, dst, row_send_sem, sem, (depth, tile)).wait_recv()

time: 27.6 us -> 23.4 us (0.85)
  Pallas kernels: 25.9 us -> 21.7 us
    pallas_call x1, Pallas kernels: 25.9 us -> 21.7 us  [render(): pl.pallas_call(functools.partial(render_kernel, depth_count, tile_count),...]
where the time goes in v3:
time: 23.4 us; the launch traced here: 23.3 us
  Pallas kernels  21.7 us (93%)
  local copies, waits for them, and re-layouts  1.57 us (7%)
    pallas_call x1, Pallas kernels, render(): pl.pallas_call(functools.partial(render_kernel, depth_count, tile_count),...  21.7 us
    unnamed x1, local copies, waits for them, and re-layouts  1.57 us

profile of v3, /device:TPU:0, one launch (start us, length us, event | category | flops | bytes accessed | tf_op | source)
XLA Modules:
  0.0 23.3 jit_solution(9865457609968288604)
XLA Ops:
  0.0 21.7 %render.1 = f32[4,32,256]{2,1,0:T(8,128)} custom-call(bf16[4,4,2,32,256]{4,3,2,1,0:T(8,128)(2,1)} %bitcast.1, f32[3,16]{1,0:T(4,128)} %color_ref.1, f32[16]{0:T(128)} %extinction_ref.1), custom_call_target="tpu_custom_call" | custom-call | tf_op jit(solution)/shard_map/render/pallas_call | solution.py:451
  21.7 1.6 %copy.5 = f32[4,32,256]{2,1,0:T(8,128)} copy(f32[4,32,256]{2,1,0:T(8,128)} %render.1) | data formatting | bytes 262144

commit v4 on v3

--- a/solution.py
+++ b/solution.py
@@ -153,8 +153,8 @@
         copy.start()
 
     barrier = pltpu.get_barrier_semaphore()
-    for step in range(1, depth_count):
-        peer = lax.rem(depth + step, depth_count)
+    for step in range(depth_count - 1, 0, -1):
+        peer = depth ^ step
         pl.semaphore_signal(barrier, inc=1, device_id=(peer, tile), device_id_type=MESH)
     for which in range(PAIR):
         for side in (left, right):
@@ -196,6 +196,89 @@
         for end in range(2):
             edge_out[end, block % PAIR, block // PAIR] = columns[end : end + 1, block * group : (block + 1) * group]
 
+    blank = jnp.zeros((pairs, 1, rows, tile_cols), jnp.bfloat16)
+
+    @pl.when(pair == 0)
+    def _():
+        slabs[:, 0:1] = blank
+
+    @pl.when(pair == pairs - 1)
+    def _():
+        slabs[:, pair_slices + 1 : pair_slices + 2] = blank
+
+    pl.semaphore_wait(barrier, depth_count - 1 + 2 * PAIR)
+
+    def remote(src, dst, sent, received, target):
+        return pltpu.make_async_remote_copy(
+            src_ref=src,
+            dst_ref=dst,
+            send_sem=sent,
+            recv_sem=received,
+            device_id=target,
+            device_id_type=MESH,
+        )
+
+    def order(step):
+        return pair ^ (pairs - 1 - step)
+
+    sends = []
+    row_in[member] = row_out[member]
+    copy = remote(
+        row_out.at[mate],
+        row_in.at[member],
+        row_send_sem,
+        row_recv_sem,
+        (pair * PAIR + mate, tile),
+    )
+    copy.start()
+    sends.append(copy)
+    for which in range(PAIR):
+        for end, beside in enumerate((left, right)):
+            copy = remote(
+                edge_out.at[end, which],
+                edge_in.at[1 - end, member],
+                edge_send_sem.at[end, which],
+                edge_recv_sem.at[1 - end, member],
+                (pair * PAIR + which, beside),
+            )
+            copy.start()
+            sends.append(copy)
+
+    def halo(which, beyond):
+        at = PAIR * local_slices + 1 if beyond < 0 else 0
+        return remote(
+            vort_hbm.at[0 if beyond < 0 else local_slices - 1, :, which],
+            slabs.at[:, at],
+            halo_send_sem.at[which],
+            halo_recv_sem.at[0 if beyond > 0 else 1],
+            ((pair + beyond) * PAIR + which, tile),
+        )
+
+    to_below = (member == 0) & (pair > 0)
+    to_above = (member == PAIR - 1) & (pair < pairs - 1)
+
+    @pl.when(to_below)
+    def _():
+        for which in range(PAIR):
+            halo(which, -1).start()
+
+    @pl.when(to_above)
+    def _():
+        for which in range(PAIR):
+            halo(which, 1).start()
+
+    for step in range(pairs):
+        chunk = order(step)
+        copy = remote(
+            vort_hbm.at[:, chunk, mate],
+            slot(chunk, member),
+            send_sem.at[step],
+            recv_sem.at[chunk],
+            (pair * PAIR + mate, tile),
+        )
+        copy.start()
+        sends.append(copy)
+
     spread = (2 + local_slices) * rows
     extra = 2 * SUBLANES
     cell = iota((group, spread + extra), 0)
@@ -243,89 +326,6 @@
             rise = jnp.take_along_axis(slope, at, axis=1, mode="promise_in_bounds")
             pieces.append(base + part[:, first : first + LANES] * rise)
         return jnp.concatenate(pieces, axis=1)
-
-    blank = jnp.zeros((pairs, 1, rows, tile_cols), jnp.bfloat16)
-
-    @pl.when(pair == 0)
-    def _():
-        slabs[:, 0:1] = blank
-
-    @pl.when(pair == pairs - 1)
-    def _():
-        slabs[:, pair_slices + 1 : pair_slices + 2] = blank
-
-    pl.semaphore_wait(barrier, depth_count - 1 + 2 * PAIR)
-
-    def remote(src, dst, sent, received, target):
-        return pltpu.make_async_remote_copy(
-            src_ref=src,
-            dst_ref=dst,
-            send_sem=sent,
-            recv_sem=received,
-            device_id=target,
-            device_id_type=MESH,
-        )
-
-    def order(step):
-        return pair ^ (pairs - 1 - step)
-
-    sends = []
-    row_in[member] = row_out[member]
-    copy = remote(
-        row_out.at[mate],
-        row_in.at[member],
-        row_send_sem,
-        row_recv_sem,
-        (pair * PAIR + mate, tile),
-    )
-    copy.start()
-    sends.append(copy)
-    for which in range(PAIR):
-        for end, beside in enumerate((left, right)):
-            copy = remote(
-                edge_out.at[end, which],
-                edge_in.at[1 - end, member],
-                edge_send_sem.at[end, which],
-                edge_recv_sem.at[1 - end, member],
-                (pair * PAIR + which, beside),
-            )
-            copy.start()
-            sends.append(copy)
-
-    def halo(which, beyond):
-        at = PAIR * local_slices + 1 if beyond < 0 else 0
-        return remote(
-            vort_hbm.at[0 if beyond < 0 else local_slices - 1, :, which],
-            slabs.at[:, at],
-            halo_send_sem.at[which],
-            halo_recv_sem.at[0 if beyond > 0 else 1],
-            ((pair + beyond) * PAIR + which, tile),
-        )
-
-    to_below = (member == 0) & (pair > 0)
-    to_above = (member == PAIR - 1) & (pair < pairs - 1)
-
-    @pl.when(to_below)
-    def _():
-        for which in range(PAIR):
-            halo(which, -1).start()
-
-    @pl.when(to_above)
-    def _():
-        for which in range(PAIR):
-            halo(which, 1).start()
-
-    for step in range(pairs):
-        chunk = order(step)
-        copy = remote(
-            vort_hbm.at[:, chunk, mate],
-            slot(chunk, member),
-            send_sem.at[step],
-            recv_sem.at[chunk],
-            (pair * PAIR + mate, tile),
-        )
-        copy.start()
-        sends.append(copy)
 
     def wait_recv(dst, sem):
         remote(dst, dst, row_send_sem, sem, (depth, tile)).wait_recv()

time: 23.4 us -> 23.4 us (level)
  no operation moved by 1% of the time
where the time goes in v4:
time: 23.4 us; the launch traced here: 23.3 us
  Pallas kernels  21.7 us (93%)
  local copies, waits for them, and re-layouts  1.57 us (7%)
    pallas_call x1, Pallas kernels, render(): pl.pallas_call(functools.partial(render_kernel, depth_count, tile_count),...  21.7 us
    unnamed x1, local copies, waits for them, and re-layouts  1.57 us

profile of v4, /device:TPU:0, one launch (start us, length us, event | category | flops | bytes accessed | tf_op | source)
XLA Modules:
  0.0 23.3 jit_solution(5246655788064596215)
XLA Ops:
  0.0 21.7 %render.1 = f32[4,32,256]{2,1,0:T(8,128)} custom-call(bf16[4,4,2,32,256]{4,3,2,1,0:T(8,128)(2,1)} %bitcast.1, f32[3,16]{1,0:T(4,128)} %color_ref.1, f32[16]{0:T(128)} %extinction_ref.1), custom_call_target="tpu_custom_call" | custom-call | tf_op jit(solution)/shard_map/render/pallas_call | solution.py:451
  21.7 1.6 %copy.5 = f32[4,32,256]{2,1,0:T(8,128)} copy(f32[4,32,256]{2,1,0:T(8,128)} %render.1) | data formatting | bytes 262144
